TPU v7x, 256 devices: a whole 4x4x8 slice. The times are simulated.
256 devices in a mesh: dp: 16 (over y, z_hi, core), tensor: 16 (over z_lo, x).
Axes of the slice: x: 4, y: 4, z: 8 (z_hi: 2, z_lo: 4; z = z_hi * 4 + z_lo), core: 2. Of those that a mesh axis runs over, the one named last changes fastest.
Arguments:
- tokens: bfloat16 [1024, 8192], P('tensor', 'dp'), may hold values from -6 to 6
- gate_weight: bfloat16 [8192, 29568], P('dp', 'tensor'), may hold values from -0.0625 to 0.0625
- up_weight: bfloat16 [8192, 29568], P('dp', 'tensor'), may hold values from -0.0625 to 0.0625
- down_weight: bfloat16 [29568, 8192], P('tensor', 'dp'), may hold values from -0.03125 to 0.03125
- labels: int32 [1024], P('tensor'), may hold values from 0 to 255
Outputs:
- erased: bfloat16 [1024, 8192], P('tensor', 'dp')
All inputs are finite; a program needn't handle non-finite values.
Results may differ from a plain program's by a relative error of at most 0.029.
Values may be sent and summed in bfloat16 or wider, within the bound.
A program may use at most 64 MiB of HBM per device.

v0:
```python
import jax
import jax.numpy as jnp
from jax import lax
from jax.sharding import PartitionSpec as P

NCLS = 256
epsilon = 1e-05
ridge_share = 0.5


def shards(tokens, gate_weight, up_weight, down_weight, labels):
    groups = lax.axis_size("tensor")
    shard_rows = tokens.shape[0]
    row_total = shard_rows * groups
    hidden_cols = gate_weight.shape[1]
    high = lax.Precision.HIGHEST
    gathered = lax.all_gather(tokens, "tensor", axis=0, tiled=True)
    joined = jnp.concatenate([gate_weight, up_weight], axis=1)
    partial_value = jnp.dot(gathered, joined, preferred_element_type=jnp.float32).astype(
        jnp.bfloat16
    )
    summed = lax.psum_scatter(
        lax.optimization_barrier(partial_value).astype(jnp.float32).astype(jnp.bfloat16),
        "dp",
        scatter_dimension=0,
        tiled=True,
    ).astype(jnp.float32)
    hidden = (jax.nn.silu(summed[:, :hidden_cols]) * summed[:, hidden_cols:]).astype(jnp.bfloat16)
    partial_out = jnp.dot(
        lax.all_gather(hidden, "dp", axis=0, tiled=True),
        down_weight,
        preferred_element_type=jnp.float32,
    )
    output = lax.psum_scatter(partial_out, "tensor", scatter_dimension=0, tiled=True)
    classes = jnp.arange(NCLS, dtype=jnp.int32)
    onehot = (labels[:, None] == classes[None, :]).astype(jnp.float32)
    col_total, counts = lax.psum((jnp.sum(output, axis=0), jnp.sum(onehot, axis=0)), "tensor")
    mean_out = col_total / row_total
    shares = counts / row_total
    centred = output - mean_out
    cross_part = jnp.dot(centred.T, onehot - shares, precision=high)
    cross_sum, square_sum = lax.psum((cross_part, jnp.sum(centred * centred, axis=0)), "tensor")
    cross = cross_sum / row_total
    variance = square_sum / row_total
    spread = jnp.sqrt(variance + epsilon)
    whitened = cross / spread[:, None]
    white_rows = centred / spread
    gram_mat, coords = lax.psum(
        (
            jnp.dot(whitened.T, whitened, precision=high),
            jnp.dot(white_rows, whitened, precision=high),
        ),
        "dp",
    )
    ridge_term = ridge_share * jnp.trace(gram_mat) / NCLS
    factor = jnp.linalg.cholesky(gram_mat + ridge_term * jnp.eye(NCLS, dtype=jnp.float32))
    solved = jax.scipy.linalg.cho_solve((factor, True), coords.T)
    correction = jnp.dot(whitened, solved, precision=high).T * spread
    return (output - correction).astype(jnp.bfloat16)


def solution(mesh):
    return jax.shard_map(
        shards,
        mesh=mesh,
        in_specs=(
            P("tensor", "dp"),
            P("dp", "tensor"),
            P("dp", "tensor"),
            P("tensor", "dp"),
            P("tensor"),
        ),
        out_specs=P("tensor", "dp"),
        check_vma=False,
    )
```

profile of v0, /device:TPU:1, one launch (start us, length us, event | category | flops | bytes accessed | tf_op | source)
XLA Modules:
  0.0 900.5 jit_solution(123671681127873409)
XLA Ops:
  7.3 76.4 %all-gather.3.cloned.1.call-done = bf16[1024,512]{1,0:T(8,128)(2,1)} async-done(((bf16[64,512]{1,0:T(8,128)(2,1)}), bf16[1024,512]{1,0:T(8,128)(2,1)}) %all-gather.3.cloned.1.call-update) | async-done | bytes 1048592 | tf_op jit(solution)/shard_map/all_gather | solution.py:17
  83.7 9.6 %convert_bitcast_fusion = bf16[1024,3696]{0,1:T(8,128)(2,1)} fusion(bf16[1024,512]{1,0:T(8,128)(2,1)} %all-gather.3.cloned.1.call-done, bf16[512,1848]{0,1:T(8,128)(2,1)} %param.7, bf16[512,1848]{0,1:T(8,128)(2,1)} %param.6), kind=kOutput, calls=%fused_computation.2 | convolution fusion | flops 3886891008 | bytes 12402688 | tf_op jit(solution)/shard_map/dot_general | solution.py:19
  93.3 10.3 %copy.34 = bf16[1024,3696]{1,0:T(8,128)(2,1)} copy(bf16[1024,3696]{0,1:T(8,128)(2,1)} %convert_bitcast_fusion) | data formatting | bytes 15138816
  103.6 138.4 %reduce-scatter.7.cloned.1.call-done = bf16[64,3696]{1,0:T(8,128)(2,1)} async-done(((bf16[1024,3696]{1,0:T(8,128)(2,1)}), bf16[64,3696]{1,0:T(8,128)(2,1)}) %reduce-scatter.7.cloned.1.call-update) | async-done | bytes 473104 | tf_op jit(solution)/shard_map/reduce_scatter | solution.py:22
  242.1 1.1 convert_element_type.23
  244.2 73.9 %all-gather.5.cloned.1.call-done = bf16[1024,1848]{1,0:T(8,128)(2,1)} async-done(((bf16[64,1848]{1,0:T(8,128)(2,1)}), bf16[1024,1848]{1,0:T(8,128)(2,1)}) %all-gather.5.cloned.1.call-update) | async-done | bytes 3784720 | tf_op jit(solution)/shard_map/all_gather | solution.py:30
  318.0 5.8 fusion.34
  324.0 73.1 %reduce-scatter.5.cloned.1.call-done = f32[64,512]{1,0:T(8,128)} async-done(((f32[1024,512]{1,0:T(8,128)}), f32[64,512]{1,0:T(8,128)}) %reduce-scatter.5.cloned.1.call-update) | async-done | bytes 131088 | tf_op jit(solution)/shard_map/reduce_scatter | solution.py:34
  398.0 31.4 %psum.42 = f32[512]{0:T(512)S(1)} all-reduce(f32[512]{0:T(512)S(1)} %reduce_sum.37), channel_id=1, replica_groups=mesh['dp'=16,'tensor'=16] {'tensor'}, use_global_device_ids=true, to_apply=%region_3.4 | all-reduce | flops 512 | bytes 4096 | tf_op jit(solution)/shard_map/psum | solution.py:37
  430.3 32.0 %all-reduce.1 = (f32[256]{0:T(256)S(1)}, f32[512]{0:T(512)S(1)}) all-reduce(f32[256]{0:T(256)S(1)} %convert_reduce_fusion, f32[512]{0:T(512)S(1)} %multiply_reduce_fusion), channel_id=1, replica_groups=mesh['dp'=16,'tensor'=16] {'tensor'}, use_global_device_ids=true, to_apply=%region_5.6 | all-reduce | flops 768 | bytes 6144 | tf_op jit(solution)/shard_map/psum | solution.py:37
  462.3 2.4 fusion.10
  464.9 173.9 %all-reduce.6.cloned.1.call-done = f32[512,256]{1,0:T(8,128)} async-done(((f32[512,256]{1,0:T(8,128)}), f32[512,256]{1,0:T(8,128)}) %all-reduce.6.cloned.1.call-update) | async-done | bytes 524304 | tf_op jit(solution)/shard_map/psum | solution.py:42
  638.8 2.2 fusion.7
  641.1 3.1 fusion.32
  644.2 182.0 %all-reduce.8.cloned.1.call-done = (f32[256,256]{0,1:T(8,128)}, f32[256,64]{0,1:T(8,128)}) async-done(((f32[256,256]{0,1:T(8,128)}, f32[256,64]{0,1:T(8,128)}), (f32[256,256]{0,1:T(8,128)}, f32[256,64]{0,1:T(8,128)})) %all-reduce.8.cloned.1.call-update) | async-done | bytes 327696 | tf_op jit(solution)/shard_map/psum | solution.py:48
  826.2 1.6 select_reduce_fusion
  830.6 11.7 %cholesky.49 = f32[128,128]{1,0:T(8,128)S(1)} custom-call(f32[128,128]{1,0:T(8,128)S(1)} %cholesky.115), custom_call_target="Cholesky" | custom-call | tf_op jit(solution)/shard_map/jit(cholesky)/cholesky | solution.py:56
  842.4 9.8 %custom-call.18 = f32[1,128,128]{1,2,0:T(8,128)S(1)} custom-call(f32[1,128,128]{2,1,0:T(8,128)S(1)} %get-tuple-element.44), custom_call_target="InvertDiagBlocksLowerTriangular" | custom-call | tf_op jit(solution)/shard_map/jit(cholesky)/cholesky | solution.py:56
  852.6 11.7 %cholesky.103 = f32[128,128]{1,0:T(8,128)S(1)} custom-call(f32[128,128]{1,0:T(8,128)S(1)} %convolution_subtract_fusion), custom_call_target="Cholesky" | custom-call | tf_op jit(solution)/shard_map/jit(cholesky)/cholesky | solution.py:56
  866.9 4.3 while.1
  867.5 1.4 dynamic-slice.7
  869.7 1.4 dynamic-slice.7
  871.3 19.7 %custom-call.19 = f32[2,128,128]{1,2,0:T(8,128)S(1)} custom-call(f32[2,128,128]{2,1,0:T(8,128)S(1)} %get-tuple-element.12), custom_call_target="InvertDiagBlocksLowerTriangular" | custom-call | tf_op jit(solution)/shard_map/jit(_cho_solve)/triangular_solve | solution.py:57
  892.3 1.3 fusion.4
  (62 shorter events, 10.6 us)
Async XLA Ops:
  6.5 311.5 %copy-start = (bf16[1848,512]{1,0:T(8,128)(2,1)S(1)}, bf16[1848,512]{1,0:T(8,128)(2,1)}, u32[]{:S(2)}) copy-start(bf16[1848,512]{1,0:T(8,128)(2,1)} %param.8) | copy-start | bytes 5677060
  6.5 77.2 %all-gather.3.cloned.1.call-start = ((), (), s32[]{:S(2)}) async-start(), calls=%async_computation.2 | async-start | bytes 1114112 | tf_op jit(solution)/shard_map/all_gather | solution.py:17
  7.3 234.8 %reduce-scatter.7.cloned.1.call-start = ((), (), s32[]{:S(2)}) async-start(), calls=%async_computation.6 | async-start | bytes 8077312 | tf_op jit(solution)/shard_map/reduce_scatter | solution.py:22
  103.6 214.4 %all-gather.5.cloned.1.call-start = ((), (), s32[]{:S(2)}) async-start(), calls=%async_computation.3 | async-start | bytes 4177920 | tf_op jit(solution)/shard_map/all_gather | solution.py:30
  244.1 79.8 %copy-start.3 = (s32[64]{0:T(128)S(1)}, s32[64]{0:T(128)}, u32[]{:S(2)}) copy-start(s32[64]{0:T(128)} %param.9) | copy-start | bytes 772
  244.1 152.9 %reduce-scatter.5.cloned.1.call-start = ((), (), s32[]{:S(2)}) async-start(), calls=%async_computation.4 | async-start | bytes 2228224 | tf_op jit(solution)/shard_map/reduce_scatter | solution.py:34
  323.8 315.0 %all-reduce.6.cloned.1.call-start = ((), (), s32[]{:S(2)}) async-start(), calls=%async_computation.5 | async-start | bytes 1048576 | tf_op jit(solution)/shard_map/psum | solution.py:42
  464.7 361.5 %all-reduce.8.cloned.1.call-start = ((), (), s32[]{:S(2)}) async-start(), calls=%async_computation.7 | async-start | bytes 655360 | tf_op jit(solution)/shard_map/psum | solution.py:48
  644.2 248.1 %copy-start.1 = (f32[64,512]{1,0:T(8,128)S(1)}, f32[64,512]{1,0:T(8,128)}, u32[]{:S(2)}) copy-start(f32[64,512]{1,0:T(8,128)} %reduce-scatter.5.cloned.1.call-done) | copy-start | bytes 393220
  644.2 248.1 %copy-start.4 = (f32[512,256]{1,0:T(8,128)S(1)}, f32[512,256]{1,0:T(8,128)}, u32[]{:S(2)}) copy-start(f32[512,256]{1,0:T(8,128)} %all-reduce.6.cloned.1.call-done) | copy-start | bytes 1572868
  826.2 64.8 %copy-start.2 = (f32[256,64]{0,1:T(8,128)S(1)}, f32[256,64]{0,1:T(8,128)}, u32[]{:S(2)}) copy-start(f32[256,64]{0,1:T(8,128)} %get-tuple-element.40) | copy-start | bytes 196612
Sparse Core Ops, SparseCore 0:
  9.1 74.5 all-gather.2
  103.7 138.3 reduce-scatter.6
  245.1 72.8 all-gather.4
  323.9 73.0 reduce-scatter.4
  464.8 173.9 all-reduce.5
  644.3 181.8 all-reduce.7
where the time goes:
time: 901 us; the launch traced here: 900 us
  waiting for transfers between devices  718 us (80%)
  blocking collectives  63.4 us (7%)
  other arithmetic  61.3 us (7%)
  matrix products  26.1 us (3%)
  between operations  15.7 us (2%)
  local copies, waits for them, and re-layouts  15.1 us (2%)
    psum x1, waiting for transfers between devices, shards(): lax.psum((jnp.dot(whitened.T, whitened, precision=high), jnp.dot(white_ro...  182 us
    psum x1, waiting for transfers between devices, shards(): lax.psum((cross_part, jnp.sum(centred * centred, axis=0)), 'tensor')  174 us
    reduce_scatter x1, waiting for transfers between devices, shards(): lax.psum_scatter(lax.optimization_barrier(partial_value).astype(jnp.float...  138 us
    all_gather x1, waiting for transfers between devices, shards(): gathered = lax.all_gather(tokens, 'tensor', axis=0, tiled=True)  76.4 us
    all_gather x1, waiting for transfers between devices, shards(): lax.all_gather(hidden, 'dp', axis=0, tiled=True)  73.9 us
    reduce_scatter x1, waiting for transfers between devices, shards(): lax.psum_scatter(partial_out, 'tensor', scatter_dimension=0, tiled=True)  73.1 us
    psum x2, blocking collectives, shards(): lax.psum((jnp.sum(output, axis=0), jnp.sum(onehot, axis=0)), 'tensor')  63.4 us
    another operation x6, other arithmetic, shards(): jnp.linalg.cholesky(gram_mat + ridge_term * jnp.eye(NCLS, dtype=jnp.float...  34 us
  transfers between devices with their start and end apart: 6, of which 6 were waited for; matrix products, arithmetic and copies ran while one was open for 0% of the time, Pallas kernels for 0%

commit v1 on v0

--- a/solution.py
+++ b/solution.py
@@ -14,7 +14,10 @@
     row_total = shard_rows * groups
     hidden_cols = gate_weight.shape[1]
     high = lax.Precision.HIGHEST
-    gathered = lax.all_gather(tokens, "tensor", axis=0, tiled=True)
+    gathered = jnp.concatenate(
+        lax.all_to_all(jnp.stack([tokens for _ in range(lax.axis_size("tensor"))]), "tensor", 0, 0),
+        axis=0,
+    )
     joined = jnp.concatenate([gate_weight, up_weight], axis=1)
     partial_value = jnp.dot(gathered, joined, preferred_element_type=jnp.float32).astype(
         jnp.bfloat16

time: 901 us -> 850 us (0.943)
  waiting for transfers between devices: 718 us -> 634 us
  blocking collectives: 63.4 us -> 97 us
    all_gather x1 -> x0, waiting for transfers between devices: 76.4 us -> none  [shards(): gathered = lax.all_gather(tokens, 'tensor', axis=0, tiled=True)]
    all_to_all x0 -> x1, blocking collectives: none -> 33.7 us  [shards(): lax.all_to_all(jnp.stack([tokens for _ in range(lax.axis_size('tensor'))]...]
  transfers between devices with their start and end apart: 6 -> 5, of which waited for: 6 -> 5; matrix products, arithmetic and copies ran while one was open for 0% -> 0% of each run, Pallas kernels for 0% -> 0%
where the time goes in v1:
time: 850 us; the launch traced here: 849 us
  waiting for transfers between devices  634 us (75%)
  blocking collectives  97 us (11%)
  other arithmetic  61.3 us (7%)
  matrix products  24.9 us (3%)
  local copies, waits for them, and re-layouts  16.2 us (2%)
  between operations  15.4 us (2%)
    psum x1, waiting for transfers between devices, shards(): lax.psum((jnp.dot(whitened.T, whitened, precision=high), jnp.dot(white_ro...  182 us
    psum x1, waiting for transfers between devices, shards(): lax.psum((cross_part, jnp.sum(centred * centred, axis=0)), 'tensor')  174 us
    reduce_scatter x1, waiting for transfers between devices, shards(): lax.psum_scatter(lax.optimization_barrier(partial_value).astype(jnp.float...  131 us
    all_gather x1, waiting for transfers between devices, shards(): lax.all_gather(hidden, 'dp', axis=0, tiled=True)  73.7 us
    reduce_scatter x1, waiting for transfers between devices, shards(): lax.psum_scatter(partial_out, 'tensor', scatter_dimension=0, tiled=True)  73.1 us
    psum x2, blocking collectives, shards(): lax.psum((jnp.sum(output, axis=0), jnp.sum(onehot, axis=0)), 'tensor')  63.4 us
    another operation x6, other arithmetic, shards(): jnp.linalg.cholesky(gram_mat + ridge_term * jnp.eye(NCLS, dtype=jnp.float...  34 us
    all_to_all x1, blocking collectives, shards(): lax.all_to_all(jnp.stack([tokens for _ in range(lax.axis_size('tensor'))]...  33.7 us
  transfers between devices with their start and end apart: 5, of which 5 were waited for; matrix products, arithmetic and copies ran while one was open for 0% of the time, Pallas kernels for 0%

profile of v1, /device:TPU:1, one launch (start us, length us, event | category | flops | bytes accessed | tf_op | source)
XLA Modules:
  0.0 848.9 jit_solution(795846868988800062)
XLA Ops:
  7.6 33.7 %all_to_all.5 = bf16[16,64,512]{2,1,0:T(8,128)(2,1)S(1)} all-to-all(bf16[16,64,512]{2,1,0:T(8,128)(2,1)S(1)} %stack.2), channel_id=1, replica_groups=mesh['dp'=16,'tensor'=16] {'tensor'}, dimensions={0} | all-to-all | bytes 2097152 | tf_op jit(solution)/shard_map/all_to_all | solution.py:18
  41.3 8.3 convert_bitcast_fusion
  49.6 10.3 %copy.34 = bf16[1024,3696]{1,0:T(8,128)(2,1)} copy(bf16[1024,3696]{0,1:T(8,128)(2,1)} %convert_bitcast_fusion) | data formatting | bytes 15138816
  60.0 131.1 %reduce-scatter.7.cloned.1.call-done = bf16[64,3696]{1,0:T(8,128)(2,1)} async-done(((bf16[1024,3696]{1,0:T(8,128)(2,1)}), bf16[64,3696]{1,0:T(8,128)(2,1)}) %reduce-scatter.7.cloned.1.call-update) | async-done | bytes 473104 | tf_op jit(solution)/shard_map/reduce_scatter | solution.py:25
  191.0 1.1 convert_element_type.23
  193.1 73.7 %all-gather.2.cloned.1.call-done = bf16[1024,1848]{1,0:T(8,128)(2,1)} async-done(((bf16[64,1848]{1,0:T(8,128)(2,1)}), bf16[1024,1848]{1,0:T(8,128)(2,1)}) %all-gather.2.cloned.1.call-update) | async-done | bytes 3784720 | tf_op jit(solution)/shard_map/all_gather | solution.py:33
  266.9 5.8 fusion.34
  272.8 73.1 %reduce-scatter.5.cloned.1.call-done = f32[64,512]{1,0:T(8,128)} async-done(((f32[1024,512]{1,0:T(8,128)}), f32[64,512]{1,0:T(8,128)}) %reduce-scatter.5.cloned.1.call-update) | async-done | bytes 131088 | tf_op jit(solution)/shard_map/reduce_scatter | solution.py:37
  346.9 31.3 %psum.42 = f32[512]{0:T(512)S(1)} all-reduce(f32[512]{0:T(512)S(1)} %reduce_sum.37), channel_id=1, replica_groups=mesh['dp'=16,'tensor'=16] {'tensor'}, use_global_device_ids=true, to_apply=%region_3.4 | all-reduce | flops 512 | bytes 4096 | tf_op jit(solution)/shard_map/psum | solution.py:40
  379.1 32.1 %all-reduce.1 = (f32[256]{0:T(256)S(1)}, f32[512]{0:T(512)S(1)}) all-reduce(f32[256]{0:T(256)S(1)} %convert_reduce_fusion, f32[512]{0:T(512)S(1)} %multiply_reduce_fusion), channel_id=1, replica_groups=mesh['dp'=16,'tensor'=16] {'tensor'}, use_global_device_ids=true, to_apply=%region_5.6 | all-reduce | flops 768 | bytes 6144 | tf_op jit(solution)/shard_map/psum | solution.py:40
  411.2 2.4 fusion.10
  413.8 173.7 %all-reduce.6.cloned.1.call-done = f32[512,256]{1,0:T(8,128)} async-done(((f32[512,256]{1,0:T(8,128)}), f32[512,256]{1,0:T(8,128)}) %all-reduce.6.cloned.1.call-update) | async-done | bytes 524304 | tf_op jit(solution)/shard_map/psum | solution.py:45
  587.5 2.2 fusion.7
  589.8 3.1 fusion.32
  592.9 182.0 %all-reduce.8.cloned.1.call-done = (f32[256,256]{0,1:T(8,128)}, f32[256,64]{0,1:T(8,128)}) async-done(((f32[256,256]{0,1:T(8,128)}, f32[256,64]{0,1:T(8,128)}), (f32[256,256]{0,1:T(8,128)}, f32[256,64]{0,1:T(8,128)})) %all-reduce.8.cloned.1.call-update) | async-done | bytes 327696 | tf_op jit(solution)/shard_map/psum | solution.py:51
  774.9 1.6 select_reduce_fusion
  779.3 11.7 %cholesky.49 = f32[128,128]{1,0:T(8,128)S(1)} custom-call(f32[128,128]{1,0:T(8,128)S(1)} %cholesky.115), custom_call_target="Cholesky" | custom-call | tf_op jit(solution)/shard_map/jit(cholesky)/cholesky | solution.py:59
  791.1 9.8 %custom-call.18 = f32[1,128,128]{1,2,0:T(8,128)S(1)} custom-call(f32[1,128,128]{2,1,0:T(8,128)S(1)} %get-tuple-element.44), custom_call_target="InvertDiagBlocksLowerTriangular" | custom-call | tf_op jit(solution)/shard_map/jit(cholesky)/cholesky | solution.py:59
  801.4 11.7 %cholesky.103 = f32[128,128]{1,0:T(8,128)S(1)} custom-call(f32[128,128]{1,0:T(8,128)S(1)} %convolution_subtract_fusion), custom_call_target="Cholesky" | custom-call | tf_op jit(solution)/shard_map/jit(cholesky)/cholesky | solution.py:59
  815.7 4.3 while.1
  816.3 1.4 dynamic-slice.7
  818.4 1.4 dynamic-slice.7
  820.0 19.7 %custom-call.19 = f32[2,128,128]{1,2,0:T(8,128)S(1)} custom-call(f32[2,128,128]{2,1,0:T(8,128)S(1)} %get-tuple-element.12), custom_call_target="InvertDiagBlocksLowerTriangular" | custom-call | tf_op jit(solution)/shard_map/jit(_cho_solve)/triangular_solve | solution.py:60
  841.0 1.3 fusion.4
  (61 shorter events, 10.9 us)
Async XLA Ops:
  6.5 260.3 %copy-start = (bf16[1848,512]{1,0:T(8,128)(2,1)S(1)}, bf16[1848,512]{1,0:T(8,128)(2,1)}, u32[]{:S(2)}) copy-start(bf16[1848,512]{1,0:T(8,128)(2,1)} %param.8) | copy-start | bytes 5677060
  6.5 184.5 %reduce-scatter.7.cloned.1.call-start = ((), (), s32[]{:S(2)}) async-start(), calls=%async_computation.6 | async-start | bytes 8077312 | tf_op jit(solution)/shard_map/reduce_scatter | solution.py:25
  59.9 206.9 %all-gather.2.cloned.1.call-start = ((), (), s32[]{:S(2)}) async-start(), calls=%async_computation.3 | async-start | bytes 4177920 | tf_op jit(solution)/shard_map/all_gather | solution.py:33
  193.1 79.7 %copy-start.3 = (s32[64]{0:T(128)S(1)}, s32[64]{0:T(128)}, u32[]{:S(2)}) copy-start(s32[64]{0:T(128)} %param.9) | copy-start | bytes 772
  193.1 152.9 %reduce-scatter.5.cloned.1.call-start = ((), (), s32[]{:S(2)}) async-start(), calls=%async_computation.4 | async-start | bytes 2228224 | tf_op jit(solution)/shard_map/reduce_scatter | solution.py:37
  272.7 314.9 %all-reduce.6.cloned.1.call-start = ((), (), s32[]{:S(2)}) async-start(), calls=%async_computation.5 | async-start | bytes 1048576 | tf_op jit(solution)/shard_map/psum | solution.py:45
  413.6 361.3 %all-reduce.8.cloned.1.call-start = ((), (), s32[]{:S(2)}) async-start(), calls=%async_computation.7 | async-start | bytes 655360 | tf_op jit(solution)/shard_map/psum | solution.py:51
  592.9 248.1 %copy-start.1 = (f32[64,512]{1,0:T(8,128)S(1)}, f32[64,512]{1,0:T(8,128)}, u32[]{:S(2)}) copy-start(f32[64,512]{1,0:T(8,128)} %reduce-scatter.5.cloned.1.call-done) | copy-start | bytes 393220
  592.9 248.1 %copy-start.4 = (f32[512,256]{1,0:T(8,128)S(1)}, f32[512,256]{1,0:T(8,128)}, u32[]{:S(2)}) copy-start(f32[512,256]{1,0:T(8,128)} %all-reduce.6.cloned.1.call-done) | copy-start | bytes 1572868
  774.9 64.8 %copy-start.2 = (f32[256,64]{0,1:T(8,128)S(1)}, f32[256,64]{0,1:T(8,128)}, u32[]{:S(2)}) copy-start(f32[256,64]{0,1:T(8,128)} %get-tuple-element.40) | copy-start | bytes 196612
Sparse Core Ops, SparseCore 0:
  60.0 130.9 reduce-scatter.6
  194.1 72.7 all-gather.1
  272.8 73.1 reduce-scatter.4
  413.7 173.7 all-reduce.5
  593.0 181.8 all-reduce.7
